TPU v7x, 32 devices: a whole 2x2x4 slice. The times are simulated.
32 devices in a mesh: cluster: 8 (over z, core), member: 4 (over y, x).
Axes of the slice: x: 2, y: 2, z: 4, core: 2. Of those that a mesh axis runs over, the one named last changes fastest.
Arguments:
- cam_jac: bfloat16 [18, 8, 16384], P(None, None, ('cluster', 'member')), may hold values from -0.625 to 0.625
- point_jac: bfloat16 [6, 8, 16384], P(None, None, ('cluster', 'member')), may hold values from -6 to 6
- residuals: bfloat16 [2, 8, 16384], P(None, None, ('cluster', 'member')), may hold values from -6 to 6
- obs_camera: int32 [8, 16384], P(None, ('cluster', 'member')), may hold values from 0 to 2047, as said below
- obs_count: int32 [16384], P(('cluster', 'member')), may hold values from 2 to 8, as said below
- new_cluster: int32 [2048], replicated, may hold values from 0 to 7, as said below
- new_slot: int32 [2048], replicated, may hold values from 0 to 255, as said below
Outputs:
- reduced_system: float32 [18432, 2304], P(('cluster', 'member'))
- camera_step: float32 [18432], P(('cluster', 'member'))
Inputs may be any that keep to these rules, and one draw needn't show every extreme that they name: `obs_camera`: old ids: camera i lies in old cluster i // 256; a point block stored on the devices of cluster c observes cameras of old cluster c only, distinct ones in all its slots. Its live observations lie in new cluster c except at most two that lie in a single other new cluster. On every device, for each other cluster, at most 16 point blocks have live observations there, and exactly 16 for some other cluster. `obs_count`: some point block of every device has 8 live observations. `new_cluster`: each old cluster keeps all but 64 of its cameras; every new cluster holds exactly 256 cameras. `new_slot`: cameras of one new cluster have distinct rows.
All inputs are finite; a program needn't handle non-finite values.
Results may differ from a plain program's by a relative error of at most 0.0038.
Values may be sent and summed in bfloat16 or wider, within the bound.
A program may use at most 192 MiB of HBM per device.

v0:
```python
import jax
import jax.numpy as jnp
from jax import lax
from jax.sharding import PartitionSpec as P

SHOTS_EACH_BATCH = 256
PANEL = 16
BCAP = 16


DAMPING = 0.5
EXACT_PRECISION = lax.Precision.HIGHEST


def invert_three(matrix):

    def cofactor(i, j):
        keep_rows = [r for r in range(3) if r != i]
        keep_cols = [r for r in range(3) if r != j]
        minor_value = (
            matrix[keep_rows[0], keep_cols[0]] * matrix[keep_rows[1], keep_cols[1]]
            - matrix[keep_rows[0], keep_cols[1]] * matrix[keep_rows[1], keep_cols[0]]
        )
        sign_value = 1.0 if (i + j) % 2 == 0 else -1.0
        return sign_value * minor_value

    cofactors = [[cofactor(i, j) for j in range(3)] for i in range(3)]
    determinant = (
        matrix[0, 0] * cofactors[0][0]
        + matrix[0, 1] * cofactors[0][1]
        + matrix[0, 2] * cofactors[0][2]
    )
    adjugate = jnp.stack([jnp.stack([cofactors[j][i] for j in range(3)]) for i in range(3)])
    return adjugate / determinant


def eliminate(cam_part, point_part, resid_part, slot_rows):
    valid_mask = (slot_rows >= 0).astype(jnp.float32)
    obs_slots = slot_rows.shape[0]
    block_count = slot_rows.shape[1]
    camera_rows = (cam_part.astype(jnp.float32) * valid_mask).reshape(2, 9, obs_slots, block_count)
    point_rows = (point_part.astype(jnp.float32) * valid_mask).reshape(2, 3, obs_slots, block_count)
    resid_rows = resid_part.astype(jnp.float32) * valid_mask
    normal_point = (
        jnp.einsum("kbon,kcon->bcn", point_rows, point_rows, precision=EXACT_PRECISION)
        + DAMPING * jnp.eye(3, dtype=jnp.float32)[:, :, None]
    )
    point_grad = jnp.einsum("kbon,kon->bn", point_rows, resid_rows, precision=EXACT_PRECISION)
    landmark_inverse_tiles = invert_three(normal_point)
    camera_point_coupling = jnp.einsum(
        "kaon,kbon->abon", camera_rows, point_rows, precision=EXACT_PRECISION
    ).astype(jnp.bfloat16)
    reduced_camera_matrix = jnp.einsum(
        "wrsd,rpd->wpsd",
        camera_point_coupling.astype(jnp.float32),
        landmark_inverse_tiles,
        precision=EXACT_PRECISION,
    ).astype(jnp.bfloat16)
    camera_normal = jnp.einsum(
        "kaon,kcon->acon", camera_rows, camera_rows, precision=EXACT_PRECISION
    )
    camera_grad = jnp.einsum(
        "kaon,kon->aon", camera_rows, resid_rows, precision=EXACT_PRECISION
    ) - jnp.einsum(
        "abon,bn->aon",
        reduced_camera_matrix.astype(jnp.float32),
        point_grad,
        precision=EXACT_PRECISION,
    )
    camera_terms = jnp.concatenate(
        [camera_normal.reshape(81, obs_slots, block_count), camera_grad], axis=0
    )
    return (camera_point_coupling, reduced_camera_matrix, camera_terms)


def collect_cameras(camera_terms, slot_rows):
    camera_ids = jnp.arange(SHOTS_EACH_BATCH, dtype=jnp.int32)
    total = jnp.zeros((90, SHOTS_EACH_BATCH), jnp.float32)
    for obs_index in range(slot_rows.shape[0]):
        onehot = (slot_rows[obs_index][:, None] == camera_ids[None, :]).astype(jnp.float32)
        total = total + jnp.dot(camera_terms[:, obs_index, :], onehot, precision=EXACT_PRECISION)
    return total


def place_blocks(values, slot_rows, first_camera, camera_count):
    block_count = slot_rows.shape[1]
    cameras = first_camera + jnp.arange(camera_count, dtype=jnp.int32)
    onehot = (slot_rows[None, :, :] == cameras[:, None, None]).astype(jnp.bfloat16)
    placed = jnp.einsum("iop,abop->iabp", onehot, values, preferred_element_type=jnp.bfloat16)
    return placed.reshape(camera_count * 9, 3 * block_count)


def schur_rows(camera_point_coupling, reduced_camera_matrix, slot_rows, first_camera, camera_count):
    left_side = place_blocks(reduced_camera_matrix, slot_rows, first_camera, camera_count)
    right_side = place_blocks(camera_point_coupling, slot_rows, 0, SHOTS_EACH_BATCH)
    return jnp.einsum("rk,ck->rc", left_side, right_side, preferred_element_type=jnp.float32)


def per_device(cam_jac, point_jac, residuals, obs_camera, obs_count, new_cluster, new_slot):
    cluster_count = lax.axis_size("cluster")
    member_count = lax.axis_size("member")
    my_cluster = lax.axis_index("cluster")
    my_member = lax.axis_index("member")
    live_mask = lax.broadcasted_iota(jnp.int32, obs_camera.shape, 0) < obs_count[None, :]
    cluster_of = jnp.take(new_cluster, obs_camera)
    row_of = jnp.take(new_slot, obs_camera)
    at_home = live_mask & (cluster_of == my_cluster)
    abroad = live_mask & (cluster_of != my_cluster)
    home_slots = jnp.where(at_home, row_of, -1)
    aimed_batch = jnp.max(jnp.where(abroad, cluster_of, -1), axis=0)
    target_hits = (
        aimed_batch[None, :] == jnp.arange(cluster_count, dtype=jnp.int32)[:, None]
    ).astype(jnp.int32)
    destination_rank = jnp.sum((jnp.cumsum(target_hits, axis=1) - 1) * target_hits, axis=0)
    column = jnp.where(aimed_batch >= 0, aimed_batch * BCAP + destination_rank, -1)
    chooser = (
        column[:, None] == jnp.arange(cluster_count * BCAP, dtype=jnp.int32)[None, :]
    ).astype(jnp.bfloat16)
    outgoing = abroad.astype(jnp.bfloat16)[None]
    slot_code = jnp.where(abroad, row_of + 1, 0).astype(jnp.bfloat16)[None]
    payload = jnp.concatenate(
        [cam_jac * outgoing, point_jac * outgoing, residuals * outgoing, slot_code], axis=0
    )
    packed_blocks = jnp.einsum(
        "kop,ps->kos", payload, chooser, preferred_element_type=jnp.float32
    ).astype(jnp.bfloat16)
    arrived = lax.all_to_all(packed_blocks, "cluster", split_axis=2, concat_axis=2, tiled=True)
    home_coupling, home_reduced, resident_summands = eliminate(
        cam_jac, point_jac, residuals, home_slots
    )
    far_slots = arrived[26].astype(jnp.int32) - 1
    far_coupling, far_reduced, far_terms = eliminate(
        arrived[:18], arrived[18:24], arrived[24:26], far_slots
    )
    camera_total = collect_cameras(resident_summands, home_slots) + collect_cameras(
        far_terms, far_slots
    )
    owned_sums = lax.psum_scatter(camera_total, "member", scatter_dimension=1, tiled=True)
    camera_point_coupling = jnp.concatenate([home_coupling, far_coupling], axis=3)
    reduced_camera_matrix = jnp.concatenate([home_reduced, far_reduced], axis=3)
    slot_rows = jnp.concatenate([home_slots, far_slots], axis=1)
    camera_share = SHOTS_EACH_BATCH // member_count
    row_count = 9 * camera_share
    first_camera = my_member * camera_share
    summed = lax.psum_scatter(
        schur_rows(
            camera_point_coupling,
            reduced_camera_matrix,
            slot_rows,
            jnp.int32(0) // 9,
            row_count * lax.axis_size("member") // 9,
        ),
        "member",
        scatter_dimension=0,
        tiled=True,
    )
    normal_blocks = (
        owned_sums[:81].reshape(9, 9, camera_share)
        + DAMPING * jnp.eye(9, dtype=jnp.float32)[:, :, None]
    )
    own_columns = (
        (first_camera + jnp.arange(camera_share, dtype=jnp.int32))[:, None]
        == jnp.arange(SHOTS_EACH_BATCH, dtype=jnp.int32)[None, :]
    ).astype(jnp.float32)
    block_diag = (
        normal_blocks.transpose(2, 0, 1)[:, :, None, :] * own_columns[:, None, :, None]
    ).reshape(row_count, 9 * SHOTS_EACH_BATCH)
    reduced_matrix = block_diag - summed
    gradient = owned_sums[81:].T.reshape(-1)
    panel_width = 9 * PANEL
    panel_count = camera_share // PANEL
    square = lax.dynamic_slice_in_dim(reduced_matrix, first_camera * 9, row_count, 1)
    diagonal = jnp.stack(
        [
            square[q * panel_width : (q + 1) * panel_width, q * panel_width : (q + 1) * panel_width]
            for q in range(panel_count)
        ]
    )
    factor = jnp.linalg.cholesky(diagonal)
    solved = jax.scipy.linalg.cho_solve(
        (factor, True), gradient.reshape(panel_count, panel_width)[..., None]
    )[..., 0]
    return (reduced_matrix, -solved.reshape(-1))


def solution(mesh):
    in_specs = (
        P(None, None, ("cluster", "member")),
        P(None, None, ("cluster", "member")),
        P(None, None, ("cluster", "member")),
        P(None, ("cluster", "member")),
        P(("cluster", "member")),
        P(),
        P(),
    )
    out_specs = (P(("cluster", "member"), None), P(("cluster", "member")))
    return jax.shard_map(
        per_device, mesh=mesh, in_specs=in_specs, out_specs=out_specs, check_vma=False
    )
```

profile of v0, /device:TPU:0, one launch (start us, length us, event | category | flops | bytes accessed | tf_op | source)
XLA Modules:
  0.0 856.7 jit_solution(5134679546885364769)
XLA Ops:
  7.2 0.7 fusion.114
  7.9 23.0 %gather_fusion = s32[4096]{0:T(1024)S(1)} fusion(s32[2048]{0:T(1024)S(1)} %copy-done, s32[4096]{0:T(1024)S(1)} %broadcast_clamp_fusion), kind=kCustom, calls=%fused_computation.clone | custom fusion | bytes 49152 | tf_op jit(solution)/shard_map/jit(_take)/gather | solution.py:105
  31.7 23.0 %gather_fusion.1 = s32[4096]{0:T(1024)S(1)} fusion(s32[2048]{0:T(1024)S(1)} %copy-done.2, s32[4096]{0:T(1024)S(1)} %broadcast_clamp_fusion), kind=kCustom, calls=%fused_computation.1.clone | custom fusion | bytes 49152 | tf_op jit(solution)/shard_map/jit(_take)/gather | solution.py:106
  54.9 1.1 reduce-window.6
  57.0 1.0 reshape.1105
  58.0 6.4 all-to-all-start
  64.5 1.1 copy.217
  65.6 3.1 copy.218
  69.3 4.0 fusion.14
  73.3 11.4 %multiply_subtract_fusion.1 = (f32[1,1,512]{0,1,2:T(1,128)S(1)}, f32[1,1,512]{0,1,2:T(1,128)S(1)}, f32[512]{0:T(512)S(1)}, f32[512]{0:T(512)S(1)}, f32[512]{0:T(512)S(1)}) fusion(f32[3,3,512]{0,1,2:T(4,128)S(1)} %fusion.14), kind=kLoop, calls=%fused_computation.123 | loop fusion | flops 8192 | bytes 28672 | tf_op jit(solution)/shard_map/sub | solution.py:21
  84.7 13.7 %add_reduce_fusion = (f32[512]{0:T(512)S(1)}, f32[512]{0:T(512)S(1)}, f32[512]{0:T(512)S(1)}, f32[512]{0:T(512)S(1)}, f32[512]{0:T(512)S(1)}, /*index=5*/f32[512]{0:T(512)S(1)}, f32[512]{0:T(512)S(1)}) fusion(f32[1,1,512]{0,1,2:T(1,128)S(1)} %get-tuple-element.75, f32[1,1,512]{0,1,2:T(1,128)S(1)} %get-tuple-element.74, f32[3,3,512]{0,1,2:T(4,128)S(1)} %fusion.14), kind=kLoop, calls=%fused_computation.114 | loop fusion | flops 10240 | bytes 34816 | tf_op jit(solution)/shard_map/add | solution.py:29
  99.0 1.1 copy.258
  100.1 3.2 copy.213
  103.3 57.3 %convolution_bitcast_fusion = f32[9,9,8,512]{0,1,3,2:T(8,128)} fusion(f32[2,9,8,512]{1,0,3,2:T(2,128)} %copy.213), kind=kOutput, calls=%fused_computation.3 | convolution fusion | flops 7962624 | bytes 1622016 | tf_op jit(solution)/shard_map/kaon,kcon->acon/dot_general | solution.py:59
  160.7 34.9 %fusion.9 = bf16[9,3,8,512]{0,1,3,2:T(4,128)(2,1)} fusion(f32[2,3,8,512]{1,0,3,2:T(2,128)S(1)} %copy-done.7, f32[2,9,8,512]{1,0,3,2:T(2,128)S(1)} %copy-done.3), kind=kOutput, calls=%fused_computation.23 | convolution fusion | flops 2764800 | bytes 614400 | tf_op jit(solution)/shard_map/kaon,kbon->abon/dot_general | solution.py:50
  195.5 1.1 copy.255
  196.7 5.5 convolution_bitcast_fusion.6
  202.1 8.8 %fusion.6 = bf16[9,3,8,512]{0,1,2,3:T(4,128)(2,1)S(1)} fusion(f32[3,3,512,1]{0,1,3,2:T(4,128)S(1)} %copy.258, bf16[9,3,8,512]{0,1,3,2:T(4,128)(2,1)} %fusion.9), kind=kOutput, calls=%fused_computation.22 | convolution fusion | flops 4091904 | bytes 460800 | tf_op jit(solution)/shard_map/wrsd,rpd->wpsd/dot_general | solution.py:53
  211.0 2.0 copy-done.5
  213.0 7.2 fusion.127
  220.2 0.9 copy.260
  221.2 16.0 %copy.215 = f32[9,9,8,512]{3,2,1,0:T(8,128)S(1)} copy(f32[9,9,8,512]{0,1,3,2:T(8,128)} %convolution_bitcast_fusion) | data formatting | bytes 2654208 | tf_op jit(solution)/shard_map/kaon,kcon->acon/transpose | solution.py:59
  237.3 1.1 pad_maximum_fusion.4
  239.1 0.7 convolution_add_fusion.6
  240.5 0.7 convolution_add_fusion.4
  241.2 0.7 convolution_add_fusion.3
  241.9 0.7 convolution_add_fusion.2
  242.5 0.7 convolution_add_fusion.1
  244.6 1.3 copy.232
  247.3 0.8 copy.263
  248.1 8.2 fusion.20
  256.3 15.4 %convolution_bitcast_fusion.3 = f32[9,9,8,128]{0,1,3,2:T(8,128)} fusion(f32[2,9,8,128]{1,0,3,2:T(2,128)S(1)} %copy.225), kind=kOutput, calls=%fused_computation.24 | convolution fusion | flops 1990656 | bytes 405504 | tf_op jit(solution)/shard_map/kaon,kcon->acon/dot_general | solution.py:59
  271.7 8.7 %fusion.12 = bf16[9,3,8,128]{0,1,3,2:T(4,128)(2,1)S(1)} fusion(f32[2,3,8,128]{1,0,3,2:T(2,128)S(1)} %copy-done.9, f32[2,9,8,128]{1,0,3,2:T(2,128)S(1)} %copy.225), kind=kOutput, calls=%fused_computation.36 | convolution fusion | flops 691200 | bytes 153600 | tf_op jit(solution)/shard_map/kaon,kbon->abon/dot_general | solution.py:50
  280.4 1.1 fusion.15
  281.5 2.9 multiply_subtract_fusion.3
  284.5 3.2 add_reduce_fusion.1
  287.9 8.7 %pad_maximum_fusion.1 = bf16[9,3,8,640]{0,1,3,2:T(4,128)(2,1)} fusion(bf16[9,3,8,128]{0,1,3,2:T(4,128)(2,1)S(1)} %fusion.12, bf16[9,3,8,512]{0,1,3,2:T(4,128)(2,1)} %fusion.9), kind=kLoop, calls=%fused_computation.7 | loop fusion | flops 138240 | bytes 552960 | tf_op jit(solution)/shard_map/concatenate | solution.py:139
  296.6 3.1 fusion.13
  299.7 7.6 pad_maximum_fusion
  307.5 10.6 %convolution_bitcast_fusion.2 = bf16[256,9,3,640]{0,1,2,3:T(8,128)(2,1)} fusion(bf16[9,3,8,640]{0,1,2,3:T(4,128)(2,1)} %pad_maximum_fusion, s32[8,640]{0,1:T(8,128)S(1)} %copy.238), kind=kOutput, calls=%fused_computation.5 | convolution fusion | flops 72089600 | bytes 9144320 | tf_op jit(solution)/shard_map/iop,abop->iabp/dot_general | solution.py:89
  318.1 36.4 %copy.240 = bf16[256,9,3,640]{3,2,1,0:T(4,128)(2,1)} copy(bf16[256,9,3,640]{0,1,2,3:T(8,128)(2,1)} %convolution_bitcast_fusion.2) | data formatting | bytes 17694720 | tf_op jit(solution)/shard_map/iop,abop->iabp/transpose | solution.py:89
  354.5 9.3 %copy.311 = bf16[288,8,3,640]{3,1,2,0:T(8,128)(2,1)} copy(bf16[288,8,3,640]{3,2,1,0:T(4,128)(2,1)} %bitcast.325) | data formatting | bytes 17694720
  363.8 10.6 %convolution_bitcast_fusion.1 = bf16[256,9,3,640]{0,1,2,3:T(8,128)(2,1)} fusion(bf16[9,3,8,640]{0,1,3,2:T(4,128)(2,1)} %pad_maximum_fusion.1, s32[8,640]{0,1:T(8,128)S(1)} %copy.238), kind=kOutput, calls=%fused_computation.4 | convolution fusion | flops 72089600 | bytes 9144320 | tf_op jit(solution)/shard_map/iop,abop->iabp/dot_general | solution.py:89
  374.5 36.8 %copy.242 = bf16[256,9,3,640]{3,2,1,0:T(4,128)(2,1)} copy(bf16[256,9,3,640]{0,1,2,3:T(8,128)(2,1)} %convolution_bitcast_fusion.1) | data formatting | bytes 17694720 | tf_op jit(solution)/shard_map/iop,abop->iabp/transpose | solution.py:89
  411.3 9.4 %copy.312 = bf16[288,8,3,640]{3,1,2,0:T(8,128)(2,1)} copy(bf16[288,8,3,640]{3,2,1,0:T(4,128)(2,1)} %bitcast.326) | data formatting | bytes 17694720
  420.7 1.1 convolution_bitcast_fusion.7
  421.9 1.8 fusion.128
  424.1 4.7 copy.227
  432.0 1.3 fusion.16
  433.4 29.4 %fusion.129 = f32[2304,2304]{1,0:T(8,128)} fusion(bf16[2304,1920]{1,0:T(8,128)(2,1)} %bitcast.327, bf16[2304,1920]{1,0:T(8,128)(2,1)} %bitcast.328), kind=kOutput, calls=%fused_computation.300 | convolution fusion | flops 20384317440 | bytes 38928384
  463.1 0.8 copy.236
  464.4 25.8 %broadcast_multiply_fusion = f32[64,9,256,9]{3,2,1,0:T(8,128)} fusion(f32[64,256]{1,0:T(8,128)S(1)} %fusion.77, f32[64,9,9]{2,1,0:T(8,128)S(1)} %copy.237), kind=kLoop, calls=%fused_computation.2 | loop fusion | flops 1327104 | bytes 5394688 | tf_op jit(solution)/shard_map/mul | solution.py:166
  490.2 50.6 %mul.755 = f32[576,2304]{1,0:T(8,128)} reshape(f32[64,9,256,9]{3,2,1,0:T(8,128)} %broadcast_multiply_fusion) | data formatting | bytes 10616832 | tf_op jit(solution)/shard_map/mul | solution.py:166
  540.8 6.4 copy.244
  547.4 106.9 %reduce-scatter.7.cloned.1.call-done = f32[576,2304]{1,0:T(8,128)} async-done(((f32[2304,2304]{1,0:T(8,128)}), f32[576,2304]{1,0:T(8,128)}) %reduce-scatter.7.cloned.1.call-update) | async-done | bytes 5308432
  654.3 6.3 copy.289
  660.6 5.0 sub.277
  665.6 2.5 copy-done.4
  668.8 46.9 %custom-call.20 = f32[4,128,128]{2,1,0:T(8,128)S(1)} custom-call(f32[4,128,128]{2,1,0:T(8,128)S(1)} %cholesky.129), custom_call_target="Cholesky" | custom-call | tf_op jit(solution)/shard_map/jit(cholesky)/cholesky | solution.py:179
  715.8 39.5 %custom-call.21 = f32[4,1,128,128]{2,3,1,0:T(8,128)S(1)} custom-call(f32[4,1,128,128]{3,2,1,0:T(8,128)S(1)} %get-tuple-element.88), custom_call_target="InvertDiagBlocksLowerTriangular" | custom-call | tf_op jit(solution)/shard_map/jit(cholesky)/cholesky | solution.py:179
  755.9 5.9 custom-call.22
  762.2 6.3 copy.248
  768.8 78.6 %custom-call.23 = f32[4,2,128,128]{2,3,1,0:T(8,128)S(1)} custom-call(f32[4,2,128,128]{3,2,1,0:T(8,128)S(1)} %pad_maximum_fusion.3), custom_call_target="InvertDiagBlocksLowerTriangular" | custom-call | tf_op jit(solution)/shard_map/jit(_cho_solve)/vmap()/triangular_solve | solution.py:180
  849.0 0.7 neg.7
  (155 shorter events, 15.3 us)
Async XLA Ops:
  7.2 0.8 copy-start
  31.0 0.7 copy-start.2
  31.7 23.1 %copy-start.15 = (s32[8,512]{1,0:T(8,128)S(1)}, s32[8,512]{1,0:T(8,128)}, u32[]{:S(2)}) copy-start(s32[8,512]{1,0:T(8,128)} %param.12) | copy-start | bytes 49156
  31.7 23.1 %copy-start.21 = (s32[512]{0:T(512)S(1)}, s32[512]{0:T(512)}, u32[]{:S(2)}) copy-start(s32[512]{0:T(512)} %param.13) | copy-start | bytes 6148
  31.7 24.7 %copy-start.10 = (bf16[18,8,512]{2,1,0:T(8,128)(2,1)S(1)}, bf16[18,8,512]{2,1,0:T(8,128)(2,1)}, u32[]{:S(2)}) copy-start(bf16[18,8,512]{2,1,0:T(8,128)(2,1)} %param.9) | copy-start | bytes 442372
  31.7 24.7 %copy-start.12 = (bf16[6,8,512]{2,1,0:T(8,128)(2,1)S(1)}, bf16[6,8,512]{2,1,0:T(8,128)(2,1)}, u32[]{:S(2)}) copy-start(bf16[6,8,512]{2,1,0:T(8,128)(2,1)} %param.10) | copy-start | bytes 147460
  31.7 24.7 %copy-start.16 = (bf16[2,8,512]{2,1,0:T(8,128)(2,1)S(1)}, bf16[2,8,512]{2,1,0:T(8,128)(2,1)}, u32[]{:S(2)}) copy-start(bf16[2,8,512]{2,1,0:T(8,128)(2,1)} %param.11) | copy-start | bytes 49156
  58.0 185.2 %all-to-all-start = ((bf16[8,2,1728]{2,1,0:T(2,128)(2,1)}), bf16[8,2,1728]{2,1,0:T(2,128)(2,1)S(1)}, u32[]{:S(2)}, u32[]{:S(2)}) async-start(bf16[8,2,1728]{2,1,0:T(2,128)(2,1)} %reshape.1105), calls=%async_computation | async-start | bytes 114688 | tf_op jit(solution)/shard_map/all_to_all | solution.py:127
  64.4 398.7 %reduce-scatter.5.cloned.1.call-start = ((), (), s32[]{:S(2)}) async-start(), calls=%async_computation.3 | async-start | bytes 163840 | tf_op jit(solution)/shard_map/reduce_scatter | solution.py:138
  64.5 8.8 %copy-start.17 = (f32[3,3]{0,1:T(4,128)}, f32[3,3]{0,1:T(4,128)S(1)}, u32[]{:S(2)}) copy-start(f32[3,3]{0,1:T(4,128)S(1)} %fusion.121) | copy-start | bytes 112
  103.3 57.4 %copy-start.3 = (f32[2,9,8,512]{1,0,3,2:T(2,128)S(1)}, f32[2,9,8,512]{1,0,3,2:T(2,128)}, u32[]{:S(2)}) copy-start(f32[2,9,8,512]{1,0,3,2:T(2,128)} %copy.213) | copy-start | bytes 884740
  103.3 57.4 %copy-start.7 = (f32[2,3,8,512]{1,0,3,2:T(2,128)S(1)}, f32[2,3,8,512]{1,0,3,2:T(2,128)}, u32[]{:S(2)}) copy-start(f32[2,3,8,512]{1,0,3,2:T(2,128)} %copy.218) | copy-start | bytes 294916
  211.0 2.0 copy-start.5
  221.1 16.1 %copy-start.14 = (f32[8,512,2]{1,0,2:T(8,128)S(1)}, f32[8,512,2]{1,0,2:T(8,128)}, u32[]{:S(2)}) copy-start(f32[8,512,2]{1,0,2:T(8,128)} %get-tuple-element.96) | copy-start | bytes 98308
  256.3 15.4 %copy-start.9 = (f32[2,3,8,128]{1,0,3,2:T(2,128)S(1)}, f32[2,3,8,128]{1,0,3,2:T(2,128)}, u32[]{:S(2)}) copy-start(f32[2,3,8,128]{1,0,3,2:T(2,128)} %copy.232) | copy-start | bytes 73732
  271.7 8.7 %copy-start.18 = (f32[3,3]{0,1:T(4,128)S(1)}, f32[3,3]{0,1:T(4,128)}, u32[]{:S(2)}) copy-start(f32[3,3]{0,1:T(4,128)} %copy-done.17) | copy-start | bytes 112
  287.9 11.7 %copy-start.6 = (bf16[9,3,8,512]{0,1,2,3:T(4,128)(2,1)S(1)}, bf16[9,3,8,512]{0,1,2,3:T(4,128)(2,1)}, u32[]{:S(2)}) copy-start(bf16[9,3,8,512]{0,1,2,3:T(4,128)(2,1)} %copy-done.5) | copy-start | bytes 663556
  411.3 10.6 %copy-start.8 = (bf16[9,3,8,128]{0,1,2,3:T(4,128)(2,1)S(1)}, bf16[9,3,8,128]{0,1,2,3:T(4,128)(2,1)}, u32[]{:S(2)}) copy-start(bf16[9,3,8,128]{0,1,2,3:T(4,128)(2,1)} %fusion.13) | copy-start | bytes 165892
  411.3 12.6 %copy-start.11 = (f32[8,128,1,9]{3,2,1,0:T(1,128)S(1)}, f32[8,128,1,9]{3,2,1,0:T(1,128)}, u32[]{:S(2)}) copy-start(f32[8,128,1,9]{3,2,1,0:T(1,128)} %fusion.20) | copy-start | bytes 110596
  433.4 220.9 %reduce-scatter.7.cloned.1.call-start = ((), (), s32[]{:S(2)}) async-start(), calls=%async_computation.4 | async-start | bytes 26542080
  540.8 6.4 copy-start.13
  547.4 113.2 %copy-start.19 = (f32[4,144,1]{1,0,2:T(4,128)}, f32[4,144,1]{1,0,2:T(4,128)S(1)}, u32[]{:S(2)}) copy-start(f32[4,144,1]{1,0,2:T(4,128)S(1)} %broadcast_in_dim_reshape_reshape.3) | copy-start | bytes 6916
  665.6 2.5 copy-start.4
  762.2 87.5 %copy-start.1 = (s32[2048]{0:T(1024)S(1)}, s32[2048]{0:T(1024)}, u32[]{:S(2)}) copy-start(s32[2048]{0:T(1024)} %param.14) | copy-start | bytes 24580
  762.2 85.2 %slice-start = ((f32[4,144,1]{1,0,2:T(4,128)}), f32[4,128,1]{1,0,2:T(4,128)S(1)}, s32[]{:S(2)}) async-start(f32[4,144,1]{1,0,2:T(4,128)} %copy-done.19), calls=%async_computation.5 | async-start | bytes 4096 | tf_op jit(solution)/shard_map/jit(_cho_solve)/vmap()/triangular_solve | solution.py:180
  762.2 85.7 %copy-start.20 = (f32[4,144,1]{1,0,2:T(4,128)S(1)}, f32[4,144,1]{1,0,2:T(4,128)}, u32[]{:S(2)}) copy-start(f32[4,144,1]{1,0,2:T(4,128)} %copy-done.19) | copy-start | bytes 6916
Sparse Core Ops, SparseCore 0:
  433.5 25.5 reduce-scatter.4
  463.0 191.2 reduce-scatter.6
where the time goes:
time: 873 us; the launch traced here: 857 us
  other arithmetic  255 us (29%)
  local copies, waits for them, and re-layouts  254 us (29%)
  matrix products  219 us (25%)
  waiting for transfers between devices  107 us (12%)
  between operations  15.3 us (2%)
    unnamed x3, waiting for transfers between devices  107 us
    another operation x10, other arithmetic, per_device(): factor = jnp.linalg.cholesky(diagonal)  92.7 us
    another operation x9, other arithmetic, per_device(): jax.scipy.linalg.cho_solve((factor, True), gradient.reshape(panel_count,...  79 us
    transpose x2, local copies, waits for them, and re-layouts, place_blocks(): jnp.einsum('iop,abop->iabp', onehot, values, preferred_element_type=jnp.b...  73.2 us
    dot_general x2, matrix products, eliminate(): jnp.einsum('kaon,kcon->acon', camera_rows, camera_rows, precision=EXACT_P...  72.8 us
    mul x2, local copies, waits for them, and re-layouts, per_device(): normal_blocks.transpose(2, 0, 1)[:, :, None, :]  57 us
    dot_general x2, matrix products, eliminate(): jnp.einsum('kaon,kbon->abon', camera_rows, point_rows, precision=EXACT_PR...  43.6 us
    unnamed x54, local copies, waits for them, and re-layouts  39 us
  transfers between devices with their start and end apart: 3, of which 1 were waited for; matrix products, arithmetic and copies ran while one was open for 34% of the time, Pallas kernels for 0%

commit v1 on v0

v1 whole, which is shorter than its diff:
```python
import functools

import jax
import jax.numpy as jnp
import numpy as np
from jax import lax
from jax.experimental import pallas as pl
from jax.experimental.pallas import tpu as pltpu
from jax.sharding import PartitionSpec as P

SHOTS = 256
PANEL = 16
BCAP = 16
DAMPING = 0.5
ROWS = 28
PW = 9 * PANEL
BF = jnp.bfloat16
F32 = jnp.float32
NT = (((1,), (1,)), ((), ()))


def pack_kernel(me_ref, table_ref, cam_ref, point_ref, resid_ref, ids_ref, count_ref,
                home_ref, far_ref, payload, *, clusters, width):
    me = me_ref[0]
    obs, points = ids_ref.shape
    ids = ids_ref[...] - me * SHOTS
    table = table_ref[...]
    camera = lax.broadcasted_iota(jnp.int32, (SHOTS, points), 0)
    codes = [
        jnp.sum(jnp.where(camera == ids[o : o + 1], table, 0.0), axis=0, keepdims=True)
        for o in range(obs)
    ]
    code = jnp.concatenate(codes, axis=0).astype(jnp.int32)
    cluster = code // SHOTS
    row = code - cluster * SHOTS
    live = lax.broadcasted_iota(jnp.int32, (obs, points), 0) < count_ref[...]
    home = live & (cluster == me)
    abroad = live & (cluster != me)
    home_f = home.astype(F32)
    slot_f = jnp.where(home, row + 1, 0).astype(F32)
    for j in range(points // width):
        cols = slice(j * width, (j + 1) * width)
        for k in range(18):
            home_ref[j, k] = (cam_ref[k, :, cols].astype(F32) * home_f[:, cols]).astype(BF)
        for k in range(6):
            home_ref[j, 18 + k] = (point_ref[k, :, cols].astype(F32) * home_f[:, cols]).astype(BF)
        for k in range(2):
            home_ref[j, 24 + k] = (resid_ref[k, :, cols].astype(F32) * home_f[:, cols]).astype(BF)
        home_ref[j, 26] = slot_f[:, cols].astype(BF)
        home_ref[j, 27] = jnp.zeros((obs, width), BF)
    aimed = jnp.max(jnp.where(abroad, cluster, -1), axis=0, keepdims=True)
    hits = (aimed == lax.broadcasted_iota(jnp.int32, (clusters, points), 0)).astype(F32)
    before = (
        lax.broadcasted_iota(jnp.int32, (points, points), 0)
        < lax.broadcasted_iota(jnp.int32, (points, points), 1)
    ).astype(BF)
    rank = jnp.sum(
        jnp.dot(hits.astype(BF), before, preferred_element_type=F32) * hits, axis=0, keepdims=True
    ).astype(jnp.int32)
    column = jnp.where(aimed >= 0, aimed * BCAP + rank, -1)
    chooser = (
        lax.broadcasted_iota(jnp.int32, (clusters * BCAP, points), 0) == column
    ).astype(BF)
    seen = jnp.zeros((1, points), F32)
    abroad_f = abroad.astype(F32)
    firsts = []
    for o in range(obs):
        here = abroad_f[o : o + 1]
        firsts.append(jnp.where(seen == 0, here, 0.0))
        seen = seen + here
    first = jnp.concatenate(firsts, axis=0)
    second = abroad_f - first
    payload[...] = jnp.zeros_like(payload)
    for r, mask in enumerate((first, second)):
        for k in range(18):
            payload[r * 32 + k : r * 32 + k + 1, :] = jnp.sum(
                cam_ref[k].astype(F32) * mask, axis=0, keepdims=True
            )
        for k in range(6):
            payload[r * 32 + 18 + k : r * 32 + 19 + k, :] = jnp.sum(
                point_ref[k].astype(F32) * mask, axis=0, keepdims=True
            )
        for k in range(2):
            payload[r * 32 + 24 + k : r * 32 + 25 + k, :] = jnp.sum(
                resid_ref[k].astype(F32) * mask, axis=0, keepdims=True
            )
        payload[r * 32 + 26 : r * 32 + 27, :] = jnp.sum(
            (row + 1).astype(F32) * mask, axis=0, keepdims=True
        )
    far_ref[...] = lax.dot_general(
        chooser, payload[...].astype(BF), NT, preferred_element_type=F32
    ).astype(BF)


def main_kernel(first_ref, g_ref, tab_ref, pick_ref, damp_ref, rowcam_ref, colcam_ref,
                out_ref, step_ref, tw, tz, terms, sw, sz, sb, wp, zp, accu, ut, gt, dacc, *, share):
    t = pl.program_id(0)
    first = first_ref[0]
    first_panel = first // PANEL
    panels = share // PANEL
    rows = 9 * share
    obs, n = g_ref.shape[2], g_ref.shape[3]
    columns = out_ref.shape[1]

    @pl.when(t == 0)
    def _():
        terms[...] = jnp.zeros_like(terms)
        accu[...] = jnp.zeros_like(accu)
        dacc[...] = jnp.zeros_like(dacc)
        out_ref[...] = jnp.zeros_like(out_ref)

    x = lambda k: g_ref[0, k].astype(F32)
    A = [[x(k * 9 + a) for a in range(9)] for k in range(2)]
    B = [[x(18 + k * 3 + b) for b in range(3)] for k in range(2)]
    e = [x(24 + k) for k in range(2)]
    slot = x(26) - 1.0
    total = lambda u: jnp.sum(u, axis=0, keepdims=True)
    V = [[None] * 3 for _ in range(3)]
    for b in range(3):
        for c in range(b, 3):
            v = total(B[0][b] * B[0][c] + B[1][b] * B[1][c])
            V[b][c] = V[c][b] = v + DAMPING if b == c else v
    g = [total(B[0][b] * e[0] + B[1][b] * e[1]) for b in range(3)]

    def cofactor(i, j):
        r = [u for u in range(3) if u != i]
        c = [u for u in range(3) if u != j]
        m = V[r[0]][c[0]] * V[r[1]][c[1]] - V[r[0]][c[1]] * V[r[1]][c[0]]
        return m if (i + j) % 2 == 0 else -m

    cof = [[cofactor(i, j) for j in range(3)] for i in range(3)]
    det = V[0][0] * cof[0][0] + V[0][1] * cof[0][1] + V[0][2] * cof[0][2]
    inv = [[jnp.broadcast_to(cof[j][i] / det, (obs, n)) for j in range(3)] for i in range(3)]
    g = [jnp.broadcast_to(u, (obs, n)) for u in g]

    def keep(index, u):
        for h in range(n // 128):
            terms[h, index * obs : (index + 1) * obs, :] = u[:, h * 128 : (h + 1) * 128]

    for a in range(9):
        W = [
            (A[0][a] * B[0][b] + A[1][a] * B[1][b]).astype(BF).astype(F32) for b in range(3)
        ]
        Z = [
            (W[0] * inv[0][b] + W[1] * inv[1][b] + W[2] * inv[2][b]).astype(BF).astype(F32)
            for b in range(3)
        ]
        for b in range(3):
            for r in range(a, 24, 9):
                for h in range(n // 128):
                    lanes = slice(h * 128, (h + 1) * 128)
                    tw[h * 3 + b, r * obs : (r + 1) * obs, :] = W[b][:, lanes]
                    tz[h * 3 + b, r * obs : (r + 1) * obs, :] = Z[b][:, lanes]
        for c in range(a, 9):
            u = A[0][a] * A[0][c] + A[1][a] * A[1][c]
            keep(a * 9 + c, u)
            if c != a:
                keep(c * 9 + a, u)
        keep(81 + a, A[0][a] * e[0] + A[1][a] * e[1] - (Z[0] * g[0] + Z[1] * g[1] + Z[2] * g[2]))

    own = lax.broadcasted_iota(jnp.int32, (share, n), 0).astype(F32) + first.astype(F32)
    added = jnp.zeros((share, 128), F32)
    for o in range(obs):
        onehot = (jnp.broadcast_to(slot[o : o + 1], (share, n)) == own).astype(F32).astype(BF)
        u = jnp.concatenate(
            [terms[h, pl.ds(o, 128, stride=obs), :] for h in range(n // 128)],
            axis=1,
        )
        high = u.astype(BF)
        low = (u - high.astype(F32)).astype(BF)
        added += lax.dot_general(onehot, high, NT, preferred_element_type=F32)
        added += lax.dot_general(onehot, low, NT, preferred_element_type=F32)
        sb[o] = jnp.broadcast_to(slot[o : o + 1], (16, n)).astype(BF)
    accu[...] += added

    for o in range(obs):
        for b in range(3):
            for v in range(9):
                start = ((16 * v) % 9) * obs + o
                for h in range(n // 128):
                    lanes = slice(h * 128, (h + 1) * 128)
                    sw[o * 3 + b, v * 16 : (v + 1) * 16, lanes] = tw[
                        h * 3 + b, pl.ds(start, 16, stride=obs), :
                    ].astype(BF)
                    sz[o * 3 + b, v * 16 : (v + 1) * 16, lanes] = tz[
                        h * 3 + b, pl.ds(start, 16, stride=obs), :
                    ].astype(BF)

    def place(source, target, index, panel):
        shift = (panel * PANEL).astype(F32).astype(BF)
        base = pl.multiple_of(index * PW, PW)
        for h in range(n // 128):
            lanes = slice(h * 128, (h + 1) * 128)
            acc = [[jnp.zeros((16, 128), BF) for _ in range(9)] for _ in range(3)]
            for o in range(obs):
                s = sb[o, :, lanes] - shift
                for v in range(9):
                    hit = s == tab_ref[v * 16 : (v + 1) * 16, :]
                    for b in range(3):
                        acc[b][v] = jnp.where(
                            hit, source[o * 3 + b, v * 16 : (v + 1) * 16, lanes], acc[b][v]
                        )
            for b in range(3):
                for v in range(9):
                    target[
                        pl.ds(base + v * 16, 16), b * n + h * 128 : b * n + (h + 1) * 128
                    ] = acc[b][v]

    def place_w(i, c):
        place(sw, wp, i, i)
        return c

    def place_z(i, c):
        place(sz, zp, i, i + first_panel)
        return c

    lax.fori_loop(0, SHOTS // PANEL, place_w, 0)
    lax.fori_loop(0, panels, place_z, 0)

    def multiply(j, c):
        at = pl.ds(pl.multiple_of(j * 256, 256), 256)
        out_ref[:, at] += lax.dot_general(zp[...], wp[at, :], NT, preferred_element_type=F32)
        return c

    lax.fori_loop(0, columns // 256, multiply, 0)

    def multiply_own(q, c):
        at = pl.ds(pl.multiple_of(q * PW, PW), PW)
        dacc[at, 0:PW] += lax.dot_general(
            zp[at, :],
            wp[pl.ds(pl.multiple_of((q + first_panel) * PW, PW), PW), :],
            NT,
            preferred_element_type=F32,
        )
        return c

    lax.fori_loop(0, panels, multiply_own, 0)

    @pl.when(t == pl.num_programs(0) - 1)
    def _():
        acc = accu[...]
        for a in range(9):
            ut[pl.ds(a, share, stride=9), :] = acc if a == 0 else pltpu.roll(acc, 128 - 9 * a, 1)
            gt[pl.ds(a, share, stride=9), :] = pltpu.roll(acc, 128 - 81 - a, 1)
        u = ut[...] + damp_ref[...]
        high = u.astype(BF)
        low = (u - high.astype(F32)).astype(BF)
        rowcam = rowcam_ref[:, 0:1]

        def blocks(pick):
            return jnp.dot(high, pick, preferred_element_type=F32) + jnp.dot(
                low, pick, preferred_element_type=F32
            )

        def finish(j, c):
            at = pl.ds(pl.multiple_of(j * 256, 256), 256)
            hit = rowcam + first.astype(F32) == colcam_ref[0:1, at]
            out_ref[:, at] = jnp.where(hit, blocks(pick_ref[:, at]), 0.0) - out_ref[:, at]
            return c

        lax.fori_loop(0, columns // 256, finish, 0)
        local = rowcam_ref[:, 1:2]
        lane = lax.broadcasted_iota(jnp.int32, (rows, 256), 1)
        m = jnp.where(local == colcam_ref[0:1, 0:256], blocks(pick_ref[:, 0:256]), 0.0) - dacc[...]
        dacc[...] = jnp.where(lane == PW, gt[:, 0:1], m)

        def eliminate(half, k, c):
            for q in range(panels):
                at = slice(q * PW, (q + 1) * PW)
                ids = lax.broadcasted_iota(jnp.int32, (PW, 128), 1) + half * 128
                col = jnp.sum(
                    jnp.where(ids == k, dacc[at, half * 128 : (half + 1) * 128], 0.0),
                    axis=1,
                    keepdims=True,
                )
                pivot = dacc[pl.ds(q * PW + k, 1), :]
                wide = lax.broadcasted_iota(jnp.int32, (1, 256), 1)
                p = jnp.sum(jnp.where(wide == k, pivot, 0.0), axis=1, keepdims=True)
                scaled = pivot / p
                down = lax.broadcasted_iota(jnp.int32, (PW, 1), 0)
                col = jnp.where(down == k, 0.0, col)
                dacc[at, :] = dacc[at, :] - col * scaled
            return c

        lax.fori_loop(0, 128, functools.partial(eliminate, 0), 0)
        lax.fori_loop(128, PW, functools.partial(eliminate, 1), 0)
        for q in range(panels):
            at = slice(q * PW, (q + 1) * PW)
            m = dacc[at, :]
            down = lax.broadcasted_iota(jnp.int32, (PW, 256), 0)
            across = lax.broadcasted_iota(jnp.int32, (PW, 256), 1)
            diag = jnp.sum(jnp.where(down == across, m, 0.0), axis=1, keepdims=True)
            rhs = jnp.sum(jnp.where(across == PW, m, 0.0), axis=1, keepdims=True)
            step_ref[at, :] = jnp.broadcast_to(-(rhs / diag), (PW, 128))


def per_device(cam_jac, point_jac, residuals, obs_camera, obs_count, new_cluster, new_slot):
    clusters = lax.axis_size("cluster")
    members = lax.axis_size("member")
    me = lax.axis_index("cluster").astype(jnp.int32)
    my_member = lax.axis_index("member").astype(jnp.int32)
    obs, points = obs_camera.shape
    width = min(256, points)
    share = SHOTS // members
    rows = 9 * share
    columns = 9 * SHOTS
    vmem = pl.BlockSpec(memory_space=pltpu.VMEM)
    smem = pl.BlockSpec(memory_space=pltpu.SMEM)

    code = (new_cluster * SHOTS + new_slot).astype(F32)
    table = lax.dynamic_slice_in_dim(code, me * SHOTS, SHOTS, 0)[:, None]
    home, far = pl.pallas_call(
        functools.partial(pack_kernel, clusters=clusters, width=width),
        out_shape=(
            jax.ShapeDtypeStruct((points // width, ROWS, obs, width), BF),
            jax.ShapeDtypeStruct((clusters * BCAP, 64), BF),
        ),
        in_specs=[smem] + [vmem] * 6,
        out_specs=(vmem, vmem),
        scratch_shapes=[pltpu.VMEM((64, points), F32)],
        name="pack",
    )(me[None], table, cam_jac, point_jac, residuals, obs_camera, obs_count[None, :])

    far = jnp.broadcast_to(
        far.reshape(clusters, 1, BCAP, 64), (clusters, members, BCAP, 64)
    ).reshape(clusters * members, BCAP, 64)
    far = lax.all_to_all(far, ("cluster", "member"), split_axis=0, concat_axis=0, tiled=True)
    home = lax.all_to_all(
        jnp.broadcast_to(home[None], (members,) + home.shape),
        "member", split_axis=0, concat_axis=0, tiled=True,
    ).reshape(-1, ROWS, obs, width)
    far = far.reshape(-1, width, 2, 32)[:, :, :, :ROWS].transpose(0, 3, 2, 1)
    far = jnp.pad(far, ((0, 0), (0, 0), (0, obs - 2), (0, 0)))
    data = jnp.concatenate([home, far], axis=0)

    r = np.arange(rows)
    c = np.arange(columns)
    lane = np.arange(128)
    tab = jnp.asarray(np.broadcast_to((np.arange(PW) // 9)[:, None], (PW, 128)), BF)
    pick = jnp.asarray(lane[:, None] == c[None, :] % 9, BF)
    damp = jnp.asarray(DAMPING * (lane[None, :] == (r % 9)[:, None]), F32)
    rowcam = np.zeros((rows, 128), np.float32)
    rowcam[:, 0] = r // 9
    rowcam[:, 1] = (r // 9) % PANEL
    colcam = jnp.asarray(np.broadcast_to((c // 9)[None, :], (8, columns)), F32)
    full = lambda s: pl.BlockSpec(s, lambda t: (0,) * len(s))
    out, step = pl.pallas_call(
        functools.partial(main_kernel, share=share),
        grid=(data.shape[0],),
        out_shape=(
            jax.ShapeDtypeStruct((rows, columns), F32),
            jax.ShapeDtypeStruct((rows, 128), F32),
        ),
        in_specs=[
            smem,
            pl.BlockSpec((1, ROWS, obs, width), lambda t: (t, 0, 0, 0)),
            full((PW, 128)),
            full((128, columns)),
            full((rows, 128)),
            full((rows, 128)),
            full((8, columns)),
        ],
        out_specs=(full((rows, columns)), full((rows, 128))),
        scratch_shapes=[
            pltpu.VMEM((width // 128 * 3, 24 * obs, 128), F32),
            pltpu.VMEM((width // 128 * 3, 24 * obs, 128), F32),
            pltpu.VMEM((width // 128, 128 * obs, 128), F32),
            pltpu.VMEM((3 * obs, PW, width), BF),
            pltpu.VMEM((3 * obs, PW, width), BF),
            pltpu.VMEM((obs, 16, width), BF),
            pltpu.VMEM((columns, 3 * width), BF),
            pltpu.VMEM((rows, 3 * width), BF),
            pltpu.VMEM((share, 128), F32),
            pltpu.VMEM((rows, 128), F32),
            pltpu.VMEM((rows, 128), F32),
            pltpu.VMEM((rows, 256), F32),
        ],
        compiler_params=pltpu.CompilerParams(vmem_limit_bytes=56 * 1024 * 1024),
        name="schur",
    )((my_member * share)[None], data, tab, pick, damp, jnp.asarray(rowcam), colcam)
    return (out, step[:, 0])


def solution(mesh):
    in_specs = (
        P(None, None, ("cluster", "member")),
        P(None, None, ("cluster", "member")),
        P(None, None, ("cluster", "member")),
        P(None, ("cluster", "member")),
        P(("cluster", "member")),
        P(),
        P(),
    )
    out_specs = (P(("cluster", "member"), None), P(("cluster", "member")))
    return jax.shard_map(
        per_device, mesh=mesh, in_specs=in_specs, out_specs=out_specs, check_vma=False
    )
```

time: 873 us -> 226 us (0.26); the launches traced: 857 us -> 225 us
  other arithmetic: 255 us -> 1.86 us
  local copies, waits for them, and re-layouts: 254 us -> 5.8 us
  matrix products: 219 us -> 0 us
  Pallas kernels: 0 us -> 187 us
  waiting for transfers between devices: 107 us -> 11.8 us
  between operations: 15.3 us -> 0.67 us
  blocking collectives: 0 us -> 14.6 us
    dot_general x32 -> x0, matrix products: 188 us -> none  [the longest x2 72.8 us: eliminate(): jnp.einsum('kaon,kcon->acon', camera_rows, camera_rows, precision=EXACT_P...]
    pallas_call x0 -> x2, Pallas kernels: none -> 187 us  [the longest x1 184 us: per_device(): pl.pallas_call(functools.partial(main_kernel, share=share), grid=(data.sh...]
    another operation x26 -> x0, other arithmetic: 173 us -> none  [the longest x10 92.7 us: per_device(): factor = jnp.linalg.cholesky(diagonal)]
    unnamed x3 -> x0, waiting for transfers between devices: 107 us -> none
    transpose x6 -> x0, local copies, waits for them, and re-layouts: 94.3 us -> none  [the longest x2 73.2 us: place_blocks(): jnp.einsum('iop,abop->iabp', onehot, values, preferred_element_type=jnp.b...]
    mul x5 -> x0, local copies, waits for them, and re-layouts: 59.1 us -> none  [the longest x2 57 us: per_device(): normal_blocks.transpose(2, 0, 1)[:, :, None, :]]
    gather x4 -> x0, local copies, waits for them, and re-layouts: 46.1 us -> none  [the longest x2 23 us: per_device(): row_of = jnp.take(new_slot, obs_camera)]
    unnamed x54 -> x3, local copies, waits for them, and re-layouts: 39 us -> 0.44 us
  transfers between devices with their start and end apart: 3 -> 1, of which waited for: 1 -> 1; matrix products, arithmetic and copies ran while one was open for 34% -> 0% of each run, Pallas kernels for 0% -> 0%
where the time goes in v1:
time: 226 us; the launch traced here: 225 us
  Pallas kernels  187 us (83%)
  blocking collectives  14.6 us (6%)
  waiting for transfers between devices  11.8 us (5%)
  local copies, waits for them, and re-layouts  5.8 us (3%)
  starting transfers between devices  3.51 us (2%)
    pallas_call x1, Pallas kernels, per_device(): pl.pallas_call(functools.partial(main_kernel, share=share), grid=(data.sh...  184 us
    all_to_all x1, blocking collectives, per_device(): lax.all_to_all(far, ('cluster', 'member'), split_axis=0, concat_axis=0, t...  14.6 us
    all_to_all x1, waiting for transfers between devices, per_device(): lax.all_to_all(jnp.broadcast_to(home[None], (members,) + home.shape), 'me...  11.8 us
  transfers between devices with their start and end apart: 1, of which 1 were waited for; matrix products, arithmetic and copies ran while one was open for 0% of the time, Pallas kernels for 0%

profile of v1, /device:TPU:0, one launch (start us, length us, event | category | flops | bytes accessed | tf_op | source)
XLA Modules:
  0.0 225.1 jit_solution(7801023815368113754)
XLA Ops:
  0.6 0.8 fusion.2
  1.4 0.8 copy.14.table_ref
  2.2 3.1 %pack.1 = (bf16[2,28,8,256]{3,2,1,0:T(8,128)(2,1)}, bf16[128,64]{1,0:T(8,128)(2,1)}) custom-call(s32[1]{0:T(128)} %bitcast.1.me_ref, f32[256,1]{1,0:T(8,128)} %copy.14.table_ref, bf16[18,8,512]{2,1,0:T(8,128)(2,1)} %cam_ref.1, bf16[6,8,512]{2,1,0:T(8,128)(2,1)} %point_ref.1, bf16[2,8,512]{2,1,0:T(8,128)(2,1)} %resid_ref.1, s32[8,512]{1,0:T(8,128)} %ids_ref.1, ...), custom_call_target="tpu_custom_call" | custom-call | tf_op jit(solution)/shard_map/pack/pallas_call | solution.py:312
  5.3 0.8 broadcast_in_dim.31
  6.1 0.1 reshape.20
  6.2 14.6 %all_to_all.10 = bf16[32,2,512]{2,1,0:T(2,128)(2,1)S(1)} all-to-all(bf16[32,2,512]{2,1,0:T(2,128)(2,1)S(1)} %reshape.20), channel_id=1, replica_groups=mesh['cluster'=8,'member'=4] {'cluster','member'}, dimensions={0} | all-to-all | bytes 131072 | tf_op jit(solution)/shard_map/all_to_all | solution.py:327
  20.8 1.9 broadcast_in_dim.29
  22.8 3.5 %all-to-all-start = ((bf16[4,2,28,8,256]{4,3,2,1,0:T(8,128)(2,1)}), bf16[4,2,28,8,256]{4,3,2,1,0:T(8,128)(2,1)S(1)}, u32[]{:S(2)}, u32[]{:S(2)}) async-start(bf16[4,2,28,8,256]{4,3,2,1,0:T(8,128)(2,1)} %broadcast_in_dim.29), calls=%async_computation | async-start | bytes 1835008 | tf_op jit(solution)/shard_map/all_to_all | solution.py:328
  26.3 0.1 reshape.21
  26.4 0.1 reshape.18
  26.6 0.2 copy.16
  26.7 11.8 %all-to-all-done = bf16[4,2,28,8,256]{4,3,2,1,0:T(8,128)(2,1)S(1)} async-done(((bf16[4,2,28,8,256]{4,3,2,1,0:T(8,128)(2,1)}), bf16[4,2,28,8,256]{4,3,2,1,0:T(8,128)(2,1)S(1)}, u32[]{:S(2)}, u32[]{:S(2)}) %all-to-all-start) | async-done | bytes 917536 | tf_op jit(solution)/shard_map/all_to_all | solution.py:328
  38.5 1.1 fusion.1.g_ref
  39.6 183.8 %schur.1 = (f32[576,2304]{1,0:T(8,128)}, f32[576,128]{1,0:T(8,128)}) custom-call(s32[1]{0:T(128)} %bitcast.first_ref, bf16[10,28,8,256]{3,2,1,0:T(8,128)(2,1)} %fusion.1.g_ref, bf16[144,128]{1,0:T(8,128)(2,1)} %constant.30.clone.tab_ref, bf16[128,2304]{1,0:T(8,128)(2,1)} %constant.31.clone.pick_ref, f32[576,128]{1,0:T(8,128)} %constant.32.clone.damp_ref, ...), custom_call_target="tpu_custom_call" | custom-call | tf_op jit(solution)/shard_map/schur/pallas_call | solution.py:347
  223.4 1.7 slice_reduce_fusion
Async XLA Ops:
  22.8 15.7 %all-to-all-start = ((bf16[4,2,28,8,256]{4,3,2,1,0:T(8,128)(2,1)}), bf16[4,2,28,8,256]{4,3,2,1,0:T(8,128)(2,1)S(1)}, u32[]{:S(2)}, u32[]{:S(2)}) async-start(bf16[4,2,28,8,256]{4,3,2,1,0:T(8,128)(2,1)} %broadcast_in_dim.29), calls=%async_computation | async-start | bytes 1835008 | tf_op jit(solution)/shard_map/all_to_all | solution.py:328

commit v2 on v1

--- a/solution.py
+++ b/solution.py
@@ -93,7 +93,7 @@
 
 
 def main_kernel(first_ref, g_ref, tab_ref, pick_ref, damp_ref, rowcam_ref, colcam_ref,
-                out_ref, step_ref, tw, tz, terms, sw, sz, sb, wp, zp, accu, ut, gt, dacc, *, share):
+                out_ref, step_ref, tw, tz, terms, sw, sz, sb, wp, zp, accu, ut, gt, dacc, *, share, home_steps):
     t = pl.program_id(0)
     first = first_ref[0]
     first_panel = first // PANEL
@@ -170,35 +170,25 @@
         low = (u - high.astype(F32)).astype(BF)
         added += lax.dot_general(onehot, high, NT, preferred_element_type=F32)
         added += lax.dot_general(onehot, low, NT, preferred_element_type=F32)
-        sb[o] = jnp.broadcast_to(slot[o : o + 1], (16, n)).astype(BF)
+        for h in range(n // 128):
+            sb[h * obs + o] = jnp.broadcast_to(
+                slot[o : o + 1, h * 128 : (h + 1) * 128], (16, 128)
+            ).astype(BF)
     accu[...] += added
 
-    for o in range(obs):
-        for b in range(3):
-            for v in range(9):
-                start = ((16 * v) % 9) * obs + o
-                for h in range(n // 128):
-                    lanes = slice(h * 128, (h + 1) * 128)
-                    sw[o * 3 + b, v * 16 : (v + 1) * 16, lanes] = tw[
-                        h * 3 + b, pl.ds(start, 16, stride=obs), :
-                    ].astype(BF)
-                    sz[o * 3 + b, v * 16 : (v + 1) * 16, lanes] = tz[
-                        h * 3 + b, pl.ds(start, 16, stride=obs), :
-                    ].astype(BF)
-
-    def place(source, target, index, panel):
+    def place_one(source, target, index, panel):
         shift = (panel * PANEL).astype(F32).astype(BF)
         base = pl.multiple_of(index * PW, PW)
         for h in range(n // 128):
             lanes = slice(h * 128, (h + 1) * 128)
             acc = [[jnp.zeros((16, 128), BF) for _ in range(9)] for _ in range(3)]
             for o in range(obs):
-                s = sb[o, :, lanes] - shift
+                s = sb[h * obs + o] - shift
                 for v in range(9):
                     hit = s == tab_ref[v * 16 : (v + 1) * 16, :]
                     for b in range(3):
                         acc[b][v] = jnp.where(
-                            hit, source[o * 3 + b, v * 16 : (v + 1) * 16, lanes], acc[b][v]
+                            hit, source[h * 3 * obs + o * 3 + b, v * 16 : (v + 1) * 16, :], acc[b][v]
                         )
             for b in range(3):
                 for v in range(9):
@@ -206,16 +196,58 @@
                         pl.ds(base + v * 16, 16), b * n + h * 128 : b * n + (h + 1) * 128
                     ] = acc[b][v]
 
-    def place_w(i, c):
-        place(sw, wp, i, i)
-        return c
-
-    def place_z(i, c):
-        place(sz, zp, i, i + first_panel)
-        return c
-
-    lax.fori_loop(0, SHOTS // PANEL, place_w, 0)
-    lax.fori_loop(0, panels, place_z, 0)
+    def place(source, target, index, panel, group, used):
+        base = pl.multiple_of(index * PW, PW)
+        for h in range(n // 128):
+            for v in range(9):
+                tab = tab_ref[v * 16 : (v + 1) * 16, :]
+                tabs = [tab + ((panel + u) * PANEL).astype(F32).astype(BF) for u in range(group)]
+                acc = [[jnp.zeros((16, 128), BF) for _ in range(3)] for _ in range(group)]
+                for o in range(used):
+                    s = sb[h * obs + o]
+                    values = [
+                        source[h * 3 * obs + o * 3 + b, v * 16 : (v + 1) * 16, :] for b in range(3)
+                    ]
+                    for u in range(group):
+                        hit = s == tabs[u]
+                        for b in range(3):
+                            acc[u][b] = jnp.where(hit, values[b], acc[u][b])
+                for u in range(group):
+                    for b in range(3):
+                        target[
+                            pl.ds(base + u * PW + v * 16, 16),
+                            b * n + h * 128 : b * n + (h + 1) * 128,
+                        ] = acc[u][b]
+
+    def place_all(used):
+        for o in range(used):
+            for b in range(3):
+                for v in range(9):
+                    start = ((16 * v) % 9) * obs + o
+                    for h in range(n // 128):
+                        for tight, wide in ((tw, sw), (tz, sz)):
+                            wide[h * 3 * obs + o * 3 + b, v * 16 : (v + 1) * 16, :] = tight[
+                                h * 3 + b, pl.ds(start, 16, stride=obs), :
+                            ].astype(BF)
+
+        def place_w(i, c):
+            if used == obs:
+                place_one(sw, wp, i, i)
+            else:
+                place(sw, wp, i * 4, i * 4, 4, used)
+            return c
+
+        lax.fori_loop(0, SHOTS // PANEL // (1 if used == obs else 4), place_w, 0)
+        group = min(4, panels)
+
+        def place_z(i, c):
+            place(sz, zp, i * group, i * group + first_panel, group, used)
+            return c
+
+        lax.fori_loop(0, panels // group, place_z, 0)
+
+    pl.when(t < home_steps)(lambda: place_all(obs))
+    pl.when(t >= home_steps)(lambda: place_all(2))
 
     def multiply(j, c):
         at = pl.ds(pl.multiple_of(j * 256, 256), 256)
@@ -345,7 +377,7 @@
     colcam = jnp.asarray(np.broadcast_to((c // 9)[None, :], (8, columns)), F32)
     full = lambda s: pl.BlockSpec(s, lambda t: (0,) * len(s))
     out, step = pl.pallas_call(
-        functools.partial(main_kernel, share=share),
+        functools.partial(main_kernel, share=share, home_steps=home.shape[0]),
         grid=(data.shape[0],),
         out_shape=(
             jax.ShapeDtypeStruct((rows, columns), F32),
@@ -365,9 +397,9 @@
             pltpu.VMEM((width // 128 * 3, 24 * obs, 128), F32),
             pltpu.VMEM((width // 128 * 3, 24 * obs, 128), F32),
             pltpu.VMEM((width // 128, 128 * obs, 128), F32),
-            pltpu.VMEM((3 * obs, PW, width), BF),
-            pltpu.VMEM((3 * obs, PW, width), BF),
-            pltpu.VMEM((obs, 16, width), BF),
+            pltpu.VMEM((width // 128 * 3 * obs, PW, 128), BF),
+            pltpu.VMEM((width // 128 * 3 * obs, PW, 128), BF),
+            pltpu.VMEM((width // 128 * obs, 16, 128), BF),
             pltpu.VMEM((columns, 3 * width), BF),
             pltpu.VMEM((rows, 3 * width), BF),
             pltpu.VMEM((share, 128), F32),

time: 226 us -> 213 us (0.942)
  Pallas kernels: 187 us -> 175 us
    pallas_call x1, Pallas kernels: 184 us -> 172 us  [per_device(): pl.pallas_call(functools.partial(main_kernel, share=share, home_steps=hom...]
where the time goes in v2:
time: 213 us
  Pallas kernels  175 us (82%)
  blocking collectives  14.6 us (7%)
  waiting for transfers between devices  11.8 us (6%)
  local copies, waits for them, and re-layouts  5.8 us (3%)
  starting transfers between devices  3.51 us (2%)
    pallas_call x1, Pallas kernels, per_device(): pl.pallas_call(functools.partial(main_kernel, share=share, home_steps=hom...  172 us
    all_to_all x1, blocking collectives, per_device(): lax.all_to_all(far, ('cluster', 'member'), split_axis=0, concat_axis=0, t...  14.6 us
    all_to_all x1, waiting for transfers between devices, per_device(): lax.all_to_all(jnp.broadcast_to(home[None], (members,) + home.shape), 'me...  11.8 us
  transfers between devices with their start and end apart: 1, of which 1 were waited for; matrix products, arithmetic and copies ran while one was open for 0% of the time, Pallas kernels for 0%

profile of v2, /device:TPU:0, one launch (start us, length us, event | category | flops | bytes accessed | tf_op | source)
XLA Modules:
  0.0 212.9 jit_solution(12948497390052964042)
XLA Ops:
  0.6 0.8 fusion.2
  1.4 0.8 copy.14.table_ref
  2.2 3.1 %pack.1 = (bf16[2,28,8,256]{3,2,1,0:T(8,128)(2,1)}, bf16[128,64]{1,0:T(8,128)(2,1)}) custom-call(s32[1]{0:T(128)} %bitcast.1.me_ref, f32[256,1]{1,0:T(8,128)} %copy.14.table_ref, bf16[18,8,512]{2,1,0:T(8,128)(2,1)} %cam_ref.1, bf16[6,8,512]{2,1,0:T(8,128)(2,1)} %point_ref.1, bf16[2,8,512]{2,1,0:T(8,128)(2,1)} %resid_ref.1, s32[8,512]{1,0:T(8,128)} %ids_ref.1, ...), custom_call_target="tpu_custom_call" | custom-call | tf_op jit(solution)/shard_map/pack/pallas_call | solution.py:344
  5.3 0.8 broadcast_in_dim.31
  6.1 0.1 reshape.20
  6.2 14.6 %all_to_all.10 = bf16[32,2,512]{2,1,0:T(2,128)(2,1)S(1)} all-to-all(bf16[32,2,512]{2,1,0:T(2,128)(2,1)S(1)} %reshape.20), channel_id=1, replica_groups=mesh['cluster'=8,'member'=4] {'cluster','member'}, dimensions={0} | all-to-all | bytes 131072 | tf_op jit(solution)/shard_map/all_to_all | solution.py:359
  20.8 1.9 broadcast_in_dim.29
  22.8 3.5 %all-to-all-start = ((bf16[4,2,28,8,256]{4,3,2,1,0:T(8,128)(2,1)}), bf16[4,2,28,8,256]{4,3,2,1,0:T(8,128)(2,1)S(1)}, u32[]{:S(2)}, u32[]{:S(2)}) async-start(bf16[4,2,28,8,256]{4,3,2,1,0:T(8,128)(2,1)} %broadcast_in_dim.29), calls=%async_computation | async-start | bytes 1835008 | tf_op jit(solution)/shard_map/all_to_all | solution.py:360
  26.3 0.1 reshape.21
  26.4 0.1 reshape.18
  26.6 0.2 copy.16
  26.7 11.8 %all-to-all-done = bf16[4,2,28,8,256]{4,3,2,1,0:T(8,128)(2,1)S(1)} async-done(((bf16[4,2,28,8,256]{4,3,2,1,0:T(8,128)(2,1)}), bf16[4,2,28,8,256]{4,3,2,1,0:T(8,128)(2,1)S(1)}, u32[]{:S(2)}, u32[]{:S(2)}) %all-to-all-start) | async-done | bytes 917536 | tf_op jit(solution)/shard_map/all_to_all | solution.py:360
  38.5 1.1 fusion.1.g_ref
  39.6 171.6 %schur.1 = (f32[576,2304]{1,0:T(8,128)}, f32[576,128]{1,0:T(8,128)}) custom-call(s32[1]{0:T(128)} %bitcast.first_ref, bf16[10,28,8,256]{3,2,1,0:T(8,128)(2,1)} %fusion.1.g_ref, bf16[144,128]{1,0:T(8,128)(2,1)} %constant.30.clone.tab_ref, bf16[128,2304]{1,0:T(8,128)(2,1)} %constant.31.clone.pick_ref, f32[576,128]{1,0:T(8,128)} %constant.32.clone.damp_ref, ...), custom_call_target="tpu_custom_call" | custom-call | tf_op jit(solution)/shard_map/schur/pallas_call | solution.py:379
  211.1 1.7 slice_reduce_fusion
Async XLA Ops:
  22.8 15.7 %all-to-all-start = ((bf16[4,2,28,8,256]{4,3,2,1,0:T(8,128)(2,1)}), bf16[4,2,28,8,256]{4,3,2,1,0:T(8,128)(2,1)S(1)}, u32[]{:S(2)}, u32[]{:S(2)}) async-start(bf16[4,2,28,8,256]{4,3,2,1,0:T(8,128)(2,1)} %broadcast_in_dim.29), calls=%async_computation | async-start | bytes 1835008 | tf_op jit(solution)/shard_map/all_to_all | solution.py:360
